TPU v7x, 768 devices: a whole 4x8x12 slice. The times are simulated.
768 devices in a mesh: dp: 16 (over y, core), expert: 48 (over z, x).
Axes of the slice: x: 4, y: 8, z: 12, core: 2. Of those that a mesh axis runs over, the one named last changes fastest.
Arguments:
- tokens: bfloat16 [98304, 3584], P(('dp', 'expert')), may hold values from -6 to 6
- route_weight: float32 [98304], P(('dp', 'expert')), may hold values from 0.1 to 1
- cotangent: bfloat16 [98304, 1024], P(('dp', 'expert')), may hold values from -6 to 6
- slot_ids: int32 [98304], P(('dp', 'expert')), may hold values from 0 to 47, as said below
- placement: int32 [48], replicated, may hold values from 0 to 39, as said below
- weight: bfloat16 [48, 3584, 1024], P('expert'), as said below
- momentum: bfloat16 [48, 3584, 1024], P('expert', 'dp'), as said below
Outputs:
- expert_out: bfloat16 [98304, 1024], P(('dp', 'expert'))
- token_grad: bfloat16 [98304, 3584], P(('dp', 'expert'))
- new_weight: bfloat16 [48, 3584, 1024], P('expert', 'dp')
- new_momentum: bfloat16 [48, 3584, 1024], P('expert', 'dp')
Inputs may be any that keep to these rules, and one draw needn't show every extreme that they name: `slot_ids`: one device's 128 tokens (an aligned block) send at most 3 tokens to one slot; in each group of 48 consecutive blocks some slot gets exactly 3 from every block. `placement`: slots j and j + 24 carry the same number for exactly 8 values of j below 24; all other slots carry distinct numbers, and every number is used. `weight`: slots with equal placement numbers hold equal matrices. `momentum`: slots with equal placement numbers hold equal matrices.
All inputs are finite; a program needn't handle non-finite values.
Results may differ from a plain program's by a relative error of at most 0.018.
Values may be sent and summed in bfloat16 or wider, within the bound.
A program may use at most 64 MiB of HBM per device.

v0:
```python
import functools

import jax
import jax.numpy as jnp
from jax import lax
from jax.experimental import pallas as pl
from jax.experimental.pallas import tpu as pltpu
from jax.sharding import PartitionSpec as P

LEARNING_RATE = 0.004
DECAY_RATE = 0.9
CAP = 3
QUARTERS = 4
MESH = pl.DeviceIdType.MESH
F32, BF16 = jnp.float32, jnp.bfloat16


def dot(a, b, dims=((1,), (0,))):
    return lax.dot_general(a, b, (dims, ((), ())), preferred_element_type=F32)


def iota(shape, axis):
    return lax.broadcasted_iota(jnp.int32, shape, axis)


class Plan:
    def __init__(self, n_dp, n_slots):
        self.nz, self.nx = (12, 4) if n_slots == 48 else (n_slots // 2, 2)
        self.ny = n_dp // 2
        self.n_slots, self.n_dp = n_slots, n_dp
        self.dp, self.me = lax.axis_index("dp"), lax.axis_index("expert")
        self.y, self.core = self.dp // 2, self.dp % 2
        self.z, self.x = self.me // self.nx, self.me % self.nx
        self.sign = 1 - 2 * self.core

    def shift(self, k):
        f = self.nz - 1 - k // self.nx
        dz = (f % 2) * ((f + 1) // 2) + (1 - f % 2) * (self.nz - f // 2)
        dx = self.nx - 1 - k % self.nx
        return dz, dx

    def peer(self, k, way):
        dz, dx = self.shift(k)
        z = (self.z + way * self.sign * dz + 2 * self.nz) % self.nz
        x = (self.x + way * self.sign * dx + 2 * self.nx) % self.nx
        return self.dp, z * self.nx + x

    def visit(self, slot):
        zs, xs = slot // self.nx, slot % self.nx
        dz = (self.sign * (zs - self.z) + 2 * self.nz) % self.nz
        dx = (self.sign * (xs - self.x) + 2 * self.nx) % self.nx
        f = jnp.where(dz == 0, 0, jnp.where(dz <= self.nz // 2, 2 * dz - 1, 2 * (self.nz - dz)))
        return (self.nz - 1 - f) * self.nx + (self.nx - 1 - dx)


def body(
    cfg,
    slot_hbm, rw_hbm, tok_hbm, cot_hbm, w_hbm,
    eo_hbm, tg_hbm, red_hbm, pbuf,
    slot_ref, rw_ref, tok_ref, cot_ref, eo_ref, tg_ref,
    wv, stk, send, recv, bsend, brecv, xbuf, gbuf, gpbuf, actbuf, dw, pr, rbuf, red,
    isem, wsem, osem, ssem, rsem, bssem, brsem, prs, prr, rss, rsr, ps, prv,
):
    plan = Plan(cfg["n_dp"], cfg["n_slots"])
    n_slots, ny = plan.n_slots, plan.ny
    tok, d = tok_ref.shape
    f = cot_ref.shape[1]
    dq, fq = d // QUARTERS, f // QUARTERS
    rows = n_slots * CAP
    chunks = cfg["chunks"]
    ft = cfg["ftile"]
    sub = dw.shape[1]

    barrier = pltpu.get_barrier_semaphore()

    def greet(k, c):
        pl.semaphore_signal(barrier, inc=1, device_id=plan.peer(k, 1), device_id_type=MESH)
        return c

    lax.fori_loop(0, n_slots - 1, greet, 0)
    up = (((plan.y + 1) % ny) * 2 + plan.core, plan.me)
    down = (((plan.y + ny - 1) % ny) * 2 + plan.core, plan.me)
    mate = (plan.y * 2 + 1 - plan.core, plan.me)
    for dev in (up, down, mate):
        pl.semaphore_signal(barrier, inc=1, device_id=dev, device_id_type=MESH)

    loads = [
        pltpu.make_async_copy(a, b, isem.at[i])
        for i, (a, b) in enumerate(
            ((slot_hbm, slot_ref), (rw_hbm, rw_ref), (tok_hbm, tok_ref), (cot_hbm, cot_ref)))
    ]
    for cp in loads:
        cp.start()
    w_copy = pltpu.make_async_copy(w_hbm, wv, wsem)
    w_copy.start()
    for cp in loads[:2]:
        cp.wait()

    srow = slot_ref[...]
    hot = (iota((n_slots, tok), 0) == srow).astype(F32)
    tri = (iota((tok, tok), 0) <= iota((tok, tok), 1)).astype(BF16)
    rank = jnp.sum(hot * (dot(hot.astype(BF16), tri) - 1.0), axis=0, keepdims=True)
    place_row = (plan.visit(srow) * CAP + rank.astype(jnp.int32)) * QUARTERS
    diag = iota((tok, tok), 0) == iota((tok, tok), 1)
    upright = lambda row: jnp.sum(jnp.where(diag, row, 0.0), axis=1, keepdims=True)
    place_col = upright(place_row.astype(F32)).astype(jnp.int32)
    rw = upright(rw_ref[...])
    for cp in loads[2:]:
        cp.wait()
    for q in range(QUARTERS):
        stk[q * tok:(q + 1) * tok, :dq] = tok_ref[:, q * dq:(q + 1) * dq]
        stk[q * tok:(q + 1) * tok, dq:] = (rw * cot_ref[:, q * fq:(q + 1) * fq].astype(F32)).astype(BF16)
    want = jnp.concatenate([place_row + q for q in range(QUARTERS)], axis=1)
    pick = jnp.where(iota((rows * QUARTERS, QUARTERS * tok), 0) == want, 1.0, 0.0).astype(BF16)
    packed = dot(pick, stk[:QUARTERS * tok]).astype(BF16).reshape(rows, QUARTERS, dq + fq)
    send[...] = packed
    recv[rows - CAP:] = packed[rows - CAP:]

    pl.semaphore_wait(barrier, n_slots - 1 + 3)

    def slab(ref, k):
        return ref.at[pl.ds(k * CAP, CAP)]

    for c, (k0, k1) in enumerate(chunks):
        def go(k, carry, c=c):
            pltpu.make_async_remote_copy(
                slab(send, k), slab(recv, k), ssem, rsem.at[c],
                device_id=plan.peer(k, 1), device_id_type=MESH).start()
            return carry

        lax.fori_loop(k0, min(k1, n_slots - 1), go, 0)

    def all_of(src, dst, s, r, k0, k1):
        span = pl.ds(k0 * CAP, (min(k1, n_slots - 1) - k0) * CAP)
        return pltpu.make_async_remote_copy(src.at[span], dst.at[span], s, r, device_id=mate, device_id_type=MESH)

    def give_back(k0, k1):
        def back(k, carry):
            pltpu.make_async_remote_copy(
                slab(bsend, k), slab(brecv, k), bssem, brsem,
                device_id=plan.peer(k, -1), device_id_type=MESH).start()
            return carry

        lax.fori_loop(k0, min(k1, n_slots - 1), back, 0)

    for c, (k0, k1) in enumerate(chunks):
        m = (k1 - k0) * CAP
        r0 = k0 * CAP
        all_of(send, recv, ssem, rsem.at[c], k0, k1).wait_recv()
        if c == 0:
            w_copy.wait()
        else:
            give_back(*chunks[c - 1])
        got = recv[r0:r0 + m].reshape(m * QUARTERS, dq + fq)
        for q in range(QUARTERS):
            shape = (m, m * QUARTERS)
            sel = jnp.where(iota(shape, 0) * QUARTERS + q == iota(shape, 1), 1.0, 0.0).astype(BF16)
            part = dot(sel, got).astype(BF16)
            xbuf[r0:r0 + m, q * dq:(q + 1) * dq] = part[:, :dq]
            gbuf[r0:r0 + m, q * fq:(q + 1) * fq] = part[:, dq:]
        for n in range(f // ft):
            cols = slice(n * ft, (n + 1) * ft)
            pre = dot(xbuf[r0:r0 + m], wv[:, cols])
            sigma = jax.nn.sigmoid(pre)
            actbuf[r0:r0 + m, cols] = (pre * sigma).astype(BF16)
            gpbuf[r0:r0 + m, cols] = (
                gbuf[r0:r0 + m, cols].astype(F32) * sigma * (1.0 + pre * (1.0 - sigma))).astype(BF16)
        gp = gpbuf[r0:r0 + m]
        for q in range(QUARTERS):
            stk[q * m:(q + 1) * m, :dq] = dot(gp, wv[q * dq:(q + 1) * dq], ((1,), (1,))).astype(BF16)
            stk[q * m:(q + 1) * m, dq:] = actbuf[r0:r0 + m, q * fq:(q + 1) * fq]
        shape = (m * QUARTERS, m * QUARTERS)
        j = iota(shape, 1)
        jq = sum((j >= m * q).astype(jnp.int32) for q in range(1, QUARTERS))
        sel = jnp.where(iota(shape, 0) == (j - jq * m) * QUARTERS + jq, 1.0, 0.0).astype(BF16)
        packed = dot(sel, stk[:m * QUARTERS]).astype(BF16).reshape(m, QUARTERS, dq + fq)
        bsend[r0:r0 + m] = packed
        if k1 == n_slots:
            brecv[rows - CAP:] = packed[m - CAP:]
    give_back(*chunks[-1])

    per = dq // sub
    for q in range(QUARTERS):
        for n in range(f // ft):
            cols = slice(n * ft, (n + 1) * ft)
            term = dot(xbuf[:, q * dq:(q + 1) * dq], gpbuf[:, cols], ((0,), (0,)))
            dw[q * per:(q + 1) * per, :, cols] = term.astype(BF16).reshape(per, sub, ft)

    owner = lambda i, h: (plan.y - i - 1 + 2 * ny) % ny if h == 0 else (plan.y + i + 1) % ny
    unit = lambda o, core, h: (o * 2 + core) * 4 + h * 2
    pairs = []
    for i in range(ny):
        for h in range(2):
            cp = pltpu.make_async_remote_copy(
                dw.at[pl.ds(unit(owner(i, h), 1 - plan.core, h), 2)],
                pr.at[i, h], prs.at[i, h], prr.at[i, h], device_id=mate, device_id_type=MESH)
            cp.start()
            pairs.append(cp)

    hops = {}
    swaps = []
    out_copies = []
    far = (plan.dp, (plan.me + n_slots // 2) % n_slots)
    for i in range(ny):
        for h in range(2):
            pairs[i * 2 + h].wait_recv()
        for s in range(2):
            for h in range(2):
                u = unit(owner(i, h), plan.core, h) + s
                val = dw[u].astype(F32) + pr[i, h, s].astype(F32)
                if i > 0:
                    hops[i - 1, h, s].wait_recv()
                    val = val + rbuf[i - 1, h, s].astype(F32)
                if i < ny - 1:
                    dw[u] = val.astype(BF16)
                    cp = pltpu.make_async_remote_copy(
                        dw.at[u], rbuf.at[i, h, s], rss.at[i, h, s], rsr.at[i, h, s],
                        device_id=up if h == 0 else down, device_id_type=MESH)
                    hops[i, h, s] = cp
                else:
                    red[h * 2 + s] = val.astype(BF16)
                    out_copies.append(pltpu.make_async_copy(red.at[h * 2 + s], red_hbm.at[h * 2 + s], osem.at[h * 2 + s]))
                    out_copies[-1].start()
                    cp = pltpu.make_async_remote_copy(
                        red.at[h * 2 + s], pbuf.at[h * 2 + s], ps.at[h * 2 + s], prv.at[h * 2 + s],
                        device_id=far, device_id_type=MESH)
                    swaps.append(cp)
                cp.start()

    all_of(bsend, brecv, bssem, brsem, 0, n_slots).wait_recv()
    back_rows = brecv[...].reshape(rows * QUARTERS, dq + fq)
    for q in range(QUARTERS):
        sel = jnp.where(iota((tok, rows * QUARTERS), 1) == place_col + q, 1.0, 0.0).astype(BF16)
        mine = dot(sel, back_rows)
        tg_ref[:, q * dq:(q + 1) * dq] = mine[:, :dq].astype(BF16)
        eo_ref[:, q * fq:(q + 1) * fq] = (rw * mine[:, dq:].astype(BF16).astype(F32)).astype(BF16)

    for i, (a, b) in enumerate(((eo_ref, eo_hbm), (tg_ref, tg_hbm))):
        out_copies.append(pltpu.make_async_copy(a, b, osem.at[4 + i]))
        out_copies[-1].start()

    all_of(send, recv, ssem, rsem.at[0], 0, n_slots).wait_send()
    all_of(bsend, brecv, bssem, brsem, 0, n_slots).wait_send()
    for cp in pairs:
        cp.wait_send()
    for cp in hops.values():
        cp.wait_send()
    for cp in out_copies:
        cp.wait()
    for cp in swaps:
        cp.wait_send()
    for cp in swaps:
        cp.wait_recv()


def finish(
    n_dp,
    place_ref, eo_in, tg_in, red_in, pbuf_in, w_hbm, mom_hbm,
    eo_out, tg_out, nw_out, nm_out,
    eov, tgv, redv, pbufv, wv, momv, nwv, nmv, isem, osem,
):
    dp, me, n_slots = lax.axis_index("dp"), lax.axis_index("expert"), place_ref.shape[1]
    share, f = momv.shape
    sub = share // 4
    ins = [
        pltpu.make_async_copy(a, b, isem.at[i])
        for i, (a, b) in enumerate((
            (tg_in, tgv), (eo_in, eov), (mom_hbm, momv),
            (w_hbm.at[pl.ds(pl.multiple_of(dp * share, 8), share)], wv), (red_in, redv), (pbuf_in, pbufv)))
    ]
    for cp in ins:
        cp.start()
    outs = [
        pltpu.make_async_copy(a, b, osem.at[i])
        for i, (a, b) in enumerate(((tgv, tg_out), (eov, eo_out), (nwv, nw_out), (nmv, nm_out)))
    ]
    labels = place_ref[...]
    lane = iota(labels.shape, 1)
    label = lambda s: jnp.sum(jnp.where(lane == s, labels, 0).astype(F32), axis=1, keepdims=True)
    same = jnp.where(label(me) == label((me + n_slots // 2) % n_slots), 1.0, 0.0)
    mask = jnp.broadcast_to(same, (sub, f)) > 0.5
    for i in range(2):
        ins[i].wait()
        outs[i].start()
    for cp in ins[2:]:
        cp.wait()
    for p in range(4):
        rs = slice(p * sub, (p + 1) * sub)
        total = redv[p].astype(F32) + jnp.where(mask, pbufv[p].astype(F32), 0.0)
        fresh = (DECAY_RATE * momv[rs].astype(F32) + total).astype(BF16)
        nmv[rs] = fresh
        nwv[rs] = (wv[rs].astype(F32) - LEARNING_RATE * fresh.astype(F32)).astype(BF16)
    for cp in outs[2:]:
        cp.start()
    for cp in outs:
        cp.wait()


CHUNKS = ((0, 24), (24, 48))


def shards(tokens, route_weight, cotangent, slot_ids, placement, weight, momentum):
    n_slots, n_dp = lax.axis_size("expert"), lax.axis_size("dp")
    tok, d = tokens.shape
    f = cotangent.shape[1]
    rows, ny = n_slots * CAP, n_dp // 2
    share = d // n_dp
    sub = share // 4
    dq, fq = d // QUARTERS, f // QUARTERS
    chunks = CHUNKS if n_slots == 48 else ((0, n_slots // 2), (n_slots // 2, n_slots))
    cfg = dict(n_dp=n_dp, n_slots=n_slots, chunks=chunks, ftile=min(f, 256))
    vmem, dma = pltpu.VMEM, pltpu.SemaphoreType.DMA
    on_chip, anywhere = pl.BlockSpec(memory_space=pltpu.VMEM), pl.BlockSpec(memory_space=pl.ANY)
    slabs = (rows, QUARTERS, dq + fq)
    shape = jax.ShapeDtypeStruct
    pieces = shape((4, sub, f), BF16)
    results = (shape((tok, f), BF16), shape((tok, d), BF16), shape((share, f), BF16), shape((share, f), BF16))
    eo, tg, red, partner = pl.pallas_call(
        functools.partial(body, cfg),
        out_shape=results[:2] + (pieces, pieces),
        in_specs=[anywhere] * 5,
        out_specs=(anywhere,) * 4,
        scratch_shapes=[
            vmem((1, tok), jnp.int32), vmem((1, tok), F32),
            vmem((tok, d), BF16), vmem((tok, f), BF16), vmem((tok, f), BF16), vmem((tok, d), BF16),
            vmem((d, f), BF16),
            vmem((QUARTERS * max(rows, tok), dq + fq), BF16),
            vmem(slabs, BF16), vmem(slabs, BF16), vmem(slabs, BF16), vmem(slabs, BF16),
            vmem((rows, d), BF16),
            vmem((rows, f), BF16), vmem((rows, f), BF16), vmem((rows, f), BF16),
            vmem((n_dp * 4, sub, f), BF16),
            vmem((ny, 2, 2, sub, f), BF16),
            vmem((ny - 1, 2, 2, sub, f), BF16),
            vmem((4, sub, f), BF16),
            dma((4,)), dma, dma((6,)), dma, dma((len(chunks),)), dma, dma,
            dma((ny, 2)), dma((ny, 2)),
            dma((ny - 1, 2, 2)), dma((ny - 1, 2, 2)),
            dma((4,)), dma((4,)),
        ],
        compiler_params=pltpu.CompilerParams(
            collective_id=0, has_side_effects=True, vmem_limit_bytes=60 * 1024 * 1024),
    )(slot_ids[None, :], route_weight[None, :], tokens, cotangent, weight[0])
    eo, tg, nw, nm = pl.pallas_call(
        functools.partial(finish, n_dp),
        out_shape=results,
        in_specs=[on_chip] + [anywhere] * 6,
        out_specs=(anywhere,) * 4,
        scratch_shapes=[
            vmem((tok, f), BF16), vmem((tok, d), BF16), vmem((4, sub, f), BF16), vmem((4, sub, f), BF16),
            vmem((share, f), BF16), vmem((share, f), BF16), vmem((share, f), BF16), vmem((share, f), BF16),
            dma((6,)), dma((4,)),
        ],
    )(placement[None, :], eo, tg, red, partner, weight[0], momentum[0])
    return eo, tg, nw[None], nm[None]


def solution(mesh):
    return jax.shard_map(
        shards,
        mesh=mesh,
        in_specs=(
            P(("dp", "expert"), None),
            P(("dp", "expert")),
            P(("dp", "expert"), None),
            P(("dp", "expert")),
            P(),
            P("expert", None, None),
            P("expert", "dp", None),
        ),
        out_specs=(
            P(("dp", "expert"), None),
            P(("dp", "expert"), None),
            P("expert", "dp", None),
            P("expert", "dp", None),
        ),
        check_vma=False,
    )
```

profile of v0, /device:TPU:1, one launch (start us, length us, event | category | flops | bytes accessed | tf_op | source)
XLA Modules:
  0.0 148.7 jit_solution(17062474800535852952)
XLA Ops:
  0.6 144.0 %shard_map.102 = (bf16[128,1024]{1,0:T(8,128)(2,1)}, bf16[128,3584]{1,0:T(8,128)(2,1)}, bf16[4,56,1024]{2,1,0:T(8,128)(2,1)}, bf16[4,56,1024]{2,1,0:T(8,128)(2,1)}) custom-call(s32[1,128]{1,0:T(1,128)} %bitcast.10, f32[1,128]{1,0:T(1,128)} %bitcast.11, bf16[128,3584]{1,0:T(8,128)(2,1)} %tok_hbm.1, bf16[128,1024]{1,0:T(8,128)(2,1)} %cot_hbm.1, ...), custom_call_target="tpu_custom_call" | custom-call | tf_op jit(solution)/shard_map/pallas_call | solution.py:318
  144.7 3.8 %shard_map.103 = (bf16[128,1024]{1,0:T(8,128)(2,1)}, bf16[128,3584]{1,0:T(8,128)(2,1)}, bf16[224,1024]{1,0:T(8,128)(2,1)}, bf16[224,1024]{1,0:T(8,128)(2,1)}) custom-call(s32[1,48]{1,0:T(1,128)} %bitcast.12, bf16[128,1024]{1,0:T(8,128)(2,1)} %get-tuple-element.12.eo_in, bf16[128,3584]{1,0:T(8,128)(2,1)} %get-tuple-element.13.tg_in, ...), custom_call_target="tpu_custom_call" | custom-call | tf_op jit(solution)/shard_map/pallas_call | solution.py:343
where the time goes:
time: 149 us
  Pallas kernels  148 us (99%)
    pallas_call x1, Pallas kernels, shards(): pl.pallas_call(functools.partial(body, cfg), out_shape=results[:2] + (pie...  144 us
    pallas_call x1, Pallas kernels, shards(): pl.pallas_call(functools.partial(finish, n_dp), out_shape=results, in_spe...  3.82 us

commit v1 on v0

--- a/solution.py
+++ b/solution.py
@@ -69,7 +69,7 @@
     rows = n_slots * CAP
     chunks = cfg["chunks"]
     ft = cfg["ftile"]
-    sub = dw.shape[1]
+    half_rows = dw.shape[2]
 
     barrier = pltpu.get_barrier_semaphore()
 
@@ -134,23 +134,12 @@
         span = pl.ds(k0 * CAP, (min(k1, n_slots - 1) - k0) * CAP)
         return pltpu.make_async_remote_copy(src.at[span], dst.at[span], s, r, device_id=mate, device_id_type=MESH)
 
-    def give_back(k0, k1):
-        def back(k, carry):
-            pltpu.make_async_remote_copy(
-                slab(bsend, k), slab(brecv, k), bssem, brsem,
-                device_id=plan.peer(k, -1), device_id_type=MESH).start()
-            return carry
-
-        lax.fori_loop(k0, min(k1, n_slots - 1), back, 0)
-
-    for c, (k0, k1) in enumerate(chunks):
-        m = (k1 - k0) * CAP
-        r0 = k0 * CAP
+    def forward(c):
+        k0, k1 = chunks[c]
+        m, r0 = (k1 - k0) * CAP, k0 * CAP
         all_of(send, recv, ssem, rsem.at[c], k0, k1).wait_recv()
         if c == 0:
             w_copy.wait()
-        else:
-            give_back(*chunks[c - 1])
         got = recv[r0:r0 + m].reshape(m * QUARTERS, dq + fq)
         for q in range(QUARTERS):
             shape = (m, m * QUARTERS)
@@ -165,6 +154,10 @@
             actbuf[r0:r0 + m, cols] = (pre * sigma).astype(BF16)
             gpbuf[r0:r0 + m, cols] = (
                 gbuf[r0:r0 + m, cols].astype(F32) * sigma * (1.0 + pre * (1.0 - sigma))).astype(BF16)
+
+    def give_back(c):
+        k0, k1 = chunks[c]
+        m, r0 = (k1 - k0) * CAP, k0 * CAP
         gp = gpbuf[r0:r0 + m]
         for q in range(QUARTERS):
             stk[q * m:(q + 1) * m, :dq] = dot(gp, wv[q * dq:(q + 1) * dq], ((1,), (1,))).astype(BF16)
@@ -177,55 +170,79 @@
         bsend[r0:r0 + m] = packed
         if k1 == n_slots:
             brecv[rows - CAP:] = packed[m - CAP:]
-    give_back(*chunks[-1])
-
-    per = dq // sub
-    for q in range(QUARTERS):
-        for n in range(f // ft):
-            cols = slice(n * ft, (n + 1) * ft)
-            term = dot(xbuf[:, q * dq:(q + 1) * dq], gpbuf[:, cols], ((0,), (0,)))
-            dw[q * per:(q + 1) * per, :, cols] = term.astype(BF16).reshape(per, sub, ft)
-
+
+    def start_back(c):
+        def back(k, carry):
+            pltpu.make_async_remote_copy(
+                slab(bsend, k), slab(brecv, k), bssem, brsem,
+                device_id=plan.peer(k, -1), device_id_type=MESH).start()
+            return carry
+
+        lax.fori_loop(chunks[c][0], min(chunks[c][1], n_slots - 1), back, 0)
+
+    last = len(chunks) - 1
+    for c in range(last):
+        forward(c)
+        give_back(c)
+        if EARLY:
+            start_back(c)
+    forward(last)
+    if not EARLY:
+        for c in range(last):
+            start_back(c)
+
+    groups = f // ft
+    per = dq // half_rows
     owner = lambda i, h: (plan.y - i - 1 + 2 * ny) % ny if h == 0 else (plan.y + i + 1) % ny
-    unit = lambda o, core, h: (o * 2 + core) * 4 + h * 2
-    pairs = []
-    for i in range(ny):
+    unit = lambda o, core, h: (o * 2 + core) * 2 + h
+    far = (plan.dp, (plan.me + n_slots // 2) % n_slots)
+    pairs, hops, swaps, out_copies = {}, {}, [], []
+
+    def term(g):
+        for q in range(QUARTERS):
+            part = dot(xbuf[:, q * dq:(q + 1) * dq], gpbuf[:, g * ft:(g + 1) * ft], ((0,), (0,)))
+            dw[g, q * per:(q + 1) * per] = part.astype(BF16).reshape(per, half_rows, ft)
+        for i in range(ny):
+            for h in range(2):
+                cp = pltpu.make_async_remote_copy(
+                    dw.at[g, unit(owner(i, h), 1 - plan.core, h)], pr.at[g, i, h], prs.at[g, i, h], prr.at[g, i, h],
+                    device_id=mate, device_id_type=MESH)
+                cp.start()
+                pairs[g, i, h] = cp
+
+    def hop(i, g):
         for h in range(2):
-            cp = pltpu.make_async_remote_copy(
-                dw.at[pl.ds(unit(owner(i, h), 1 - plan.core, h), 2)],
-                pr.at[i, h], prs.at[i, h], prr.at[i, h], device_id=mate, device_id_type=MESH)
+            u = unit(owner(i, h), plan.core, h)
+            pairs[g, i, h].wait_recv()
+            val = dw[g, u].astype(F32) + pr[g, i, h].astype(F32)
+            if i > 0:
+                hops[i - 1, g, h].wait_recv()
+                val = val + rbuf[g, i - 1, h].astype(F32)
+            if i < ny - 1:
+                dw[g, u] = val.astype(BF16)
+                cp = pltpu.make_async_remote_copy(
+                    dw.at[g, u], rbuf.at[g, i, h], rss.at[g, i, h], rsr.at[g, i, h],
+                    device_id=up if h == 0 else down, device_id_type=MESH)
+                hops[i, g, h] = cp
+            else:
+                red[h, g] = val.astype(BF16)
+                out_copies.append(pltpu.make_async_copy(red.at[h, g], red_hbm.at[h, g], osem.at[2 + h * groups + g]))
+                out_copies[-1].start()
+                cp = pltpu.make_async_remote_copy(
+                    red.at[h, g], pbuf.at[h, g], ps.at[h, g], prv.at[h, g], device_id=far, device_id_type=MESH)
+                swaps.append(cp)
             cp.start()
-            pairs.append(cp)
-
-    hops = {}
-    swaps = []
-    out_copies = []
-    far = (plan.dp, (plan.me + n_slots // 2) % n_slots)
-    for i in range(ny):
-        for h in range(2):
-            pairs[i * 2 + h].wait_recv()
-        for s in range(2):
-            for h in range(2):
-                u = unit(owner(i, h), plan.core, h) + s
-                val = dw[u].astype(F32) + pr[i, h, s].astype(F32)
-                if i > 0:
-                    hops[i - 1, h, s].wait_recv()
-                    val = val + rbuf[i - 1, h, s].astype(F32)
-                if i < ny - 1:
-                    dw[u] = val.astype(BF16)
-                    cp = pltpu.make_async_remote_copy(
-                        dw.at[u], rbuf.at[i, h, s], rss.at[i, h, s], rsr.at[i, h, s],
-                        device_id=up if h == 0 else down, device_id_type=MESH)
-                    hops[i, h, s] = cp
-                else:
-                    red[h * 2 + s] = val.astype(BF16)
-                    out_copies.append(pltpu.make_async_copy(red.at[h * 2 + s], red_hbm.at[h * 2 + s], osem.at[h * 2 + s]))
-                    out_copies[-1].start()
-                    cp = pltpu.make_async_remote_copy(
-                        red.at[h * 2 + s], pbuf.at[h * 2 + s], ps.at[h * 2 + s], prv.at[h * 2 + s],
-                        device_id=far, device_id_type=MESH)
-                    swaps.append(cp)
-                cp.start()
+
+    term(0)
+    for g in range(1, groups):
+        term(g)
+        hop(0, g - 1)
+    hop(0, groups - 1)
+    give_back(last)
+    start_back(last)
+    for i in range(1, ny):
+        for g in range(groups):
+            hop(i, g)
 
     all_of(bsend, brecv, bssem, brsem, 0, n_slots).wait_recv()
     back_rows = brecv[...].reshape(rows * QUARTERS, dq + fq)
@@ -236,12 +253,12 @@
         eo_ref[:, q * fq:(q + 1) * fq] = (rw * mine[:, dq:].astype(BF16).astype(F32)).astype(BF16)
 
     for i, (a, b) in enumerate(((eo_ref, eo_hbm), (tg_ref, tg_hbm))):
-        out_copies.append(pltpu.make_async_copy(a, b, osem.at[4 + i]))
+        out_copies.append(pltpu.make_async_copy(a, b, osem.at[i]))
         out_copies[-1].start()
 
     all_of(send, recv, ssem, rsem.at[0], 0, n_slots).wait_send()
     all_of(bsend, brecv, bssem, brsem, 0, n_slots).wait_send()
-    for cp in pairs:
+    for cp in pairs.values():
         cp.wait_send()
     for cp in hops.values():
         cp.wait_send()
@@ -257,45 +274,48 @@
     n_dp,
     place_ref, eo_in, tg_in, red_in, pbuf_in, w_hbm, mom_hbm,
     eo_out, tg_out, nw_out, nm_out,
-    eov, tgv, redv, pbufv, wv, momv, nwv, nmv, isem, osem,
+    eov, tgv, redv, pbufv, wv, momv, nwv, nmv, isem, tsem, osem,
 ):
     dp, me, n_slots = lax.axis_index("dp"), lax.axis_index("expert"), place_ref.shape[1]
-    share, f = momv.shape
-    sub = share // 4
-    ins = [
-        pltpu.make_async_copy(a, b, isem.at[i])
-        for i, (a, b) in enumerate((
-            (tg_in, tgv), (eo_in, eov), (mom_hbm, momv),
-            (w_hbm.at[pl.ds(pl.multiple_of(dp * share, 8), share)], wv), (red_in, redv), (pbuf_in, pbufv)))
-    ]
-    for cp in ins:
+    _, groups, half, ft = redv.shape
+    row0 = dp * 2 * half
+    ins = {}
+    for h in range(2):
+        old = w_hbm.at[pl.ds(pl.multiple_of(row0 + h * half, 8), half)]
+        for j, (a, b) in enumerate((
+            (red_in.at[h], redv.at[h]), (pbuf_in.at[h], pbufv.at[h]), (mom_hbm.at[pl.ds(h * half, half)], momv.at[h]), (old, wv.at[h]))):
+            ins[h, j] = pltpu.make_async_copy(a, b, isem.at[h, j])
+            ins[h, j].start()
+    whole = [pltpu.make_async_copy(a, b, tsem.at[i]) for i, (a, b) in enumerate(((tg_in, tgv), (eo_in, eov)))]
+    for cp in whole:
         cp.start()
-    outs = [
-        pltpu.make_async_copy(a, b, osem.at[i])
-        for i, (a, b) in enumerate(((tgv, tg_out), (eov, eo_out), (nwv, nw_out), (nmv, nm_out)))
-    ]
+    outs = [pltpu.make_async_copy(a, b, osem.at[i]) for i, (a, b) in enumerate(((tgv, tg_out), (eov, eo_out)))]
     labels = place_ref[...]
     lane = iota(labels.shape, 1)
     label = lambda s: jnp.sum(jnp.where(lane == s, labels, 0).astype(F32), axis=1, keepdims=True)
     same = jnp.where(label(me) == label((me + n_slots // 2) % n_slots), 1.0, 0.0)
-    mask = jnp.broadcast_to(same, (sub, f)) > 0.5
-    for i in range(2):
-        ins[i].wait()
-        outs[i].start()
-    for cp in ins[2:]:
-        cp.wait()
-    for p in range(4):
-        rs = slice(p * sub, (p + 1) * sub)
-        total = redv[p].astype(F32) + jnp.where(mask, pbufv[p].astype(F32), 0.0)
-        fresh = (DECAY_RATE * momv[rs].astype(F32) + total).astype(BF16)
-        nmv[rs] = fresh
-        nwv[rs] = (wv[rs].astype(F32) - LEARNING_RATE * fresh.astype(F32)).astype(BF16)
-    for cp in outs[2:]:
-        cp.start()
+    mask = jnp.broadcast_to(same, (half, ft)) > 0.5
+    for h in range(2):
+        for j in range(4):
+            ins[h, j].wait()
+        for g in range(groups):
+            cols = slice(g * ft, (g + 1) * ft)
+            total = redv[h, g].astype(F32) + jnp.where(mask, pbufv[h, g].astype(F32), 0.0)
+            fresh = (DECAY_RATE * momv[h, :, cols].astype(F32) + total).astype(BF16)
+            nmv[h, :, cols] = fresh
+            nwv[h, :, cols] = (wv[h, :, cols].astype(F32) - LEARNING_RATE * fresh.astype(F32)).astype(BF16)
+        for j, (a, b) in enumerate(((nmv, nm_out), (nwv, nw_out))):
+            outs.append(pltpu.make_async_copy(a.at[h], b.at[pl.ds(h * half, half)], osem.at[2 + h * 2 + j]))
+            outs[-1].start()
+        if h == 0:
+            for i in range(2):
+                whole[i].wait()
+                outs[i].start()
     for cp in outs:
         cp.wait()
 
 
+EARLY = True
 CHUNKS = ((0, 24), (24, 48))
 
 
@@ -305,15 +325,16 @@
     f = cotangent.shape[1]
     rows, ny = n_slots * CAP, n_dp // 2
     share = d // n_dp
-    sub = share // 4
+    half, ft = share // 2, min(f, 256)
+    groups = f // ft
     dq, fq = d // QUARTERS, f // QUARTERS
     chunks = CHUNKS if n_slots == 48 else ((0, n_slots // 2), (n_slots // 2, n_slots))
-    cfg = dict(n_dp=n_dp, n_slots=n_slots, chunks=chunks, ftile=min(f, 256))
+    cfg = dict(n_dp=n_dp, n_slots=n_slots, chunks=chunks, ftile=ft)
     vmem, dma = pltpu.VMEM, pltpu.SemaphoreType.DMA
     on_chip, anywhere = pl.BlockSpec(memory_space=pltpu.VMEM), pl.BlockSpec(memory_space=pl.ANY)
     slabs = (rows, QUARTERS, dq + fq)
     shape = jax.ShapeDtypeStruct
-    pieces = shape((4, sub, f), BF16)
+    pieces = shape((2, groups, half, ft), BF16)
     results = (shape((tok, f), BF16), shape((tok, d), BF16), shape((share, f), BF16), shape((share, f), BF16))
     eo, tg, red, partner = pl.pallas_call(
         functools.partial(body, cfg),
@@ -328,14 +349,14 @@
             vmem(slabs, BF16), vmem(slabs, BF16), vmem(slabs, BF16), vmem(slabs, BF16),
             vmem((rows, d), BF16),
             vmem((rows, f), BF16), vmem((rows, f), BF16), vmem((rows, f), BF16),
-            vmem((n_dp * 4, sub, f), BF16),
-            vmem((ny, 2, 2, sub, f), BF16),
-            vmem((ny - 1, 2, 2, sub, f), BF16),
-            vmem((4, sub, f), BF16),
-            dma((4,)), dma, dma((6,)), dma, dma((len(chunks),)), dma, dma,
-            dma((ny, 2)), dma((ny, 2)),
-            dma((ny - 1, 2, 2)), dma((ny - 1, 2, 2)),
-            dma((4,)), dma((4,)),
+            vmem((groups, n_dp * 2, half, ft), BF16),
+            vmem((groups, ny, 2, half, ft), BF16),
+            vmem((groups, ny - 1, 2, half, ft), BF16),
+            vmem((2, groups, half, ft), BF16),
+            dma((4,)), dma, dma((2 + 2 * groups,)), dma, dma((len(chunks),)), dma, dma,
+            dma((groups, ny, 2)), dma((groups, ny, 2)),
+            dma((groups, ny - 1, 2)), dma((groups, ny - 1, 2)),
+            dma((2, groups)), dma((2, groups)),
         ],
         compiler_params=pltpu.CompilerParams(
             collective_id=0, has_side_effects=True, vmem_limit_bytes=60 * 1024 * 1024),
@@ -346,9 +367,9 @@
         in_specs=[on_chip] + [anywhere] * 6,
         out_specs=(anywhere,) * 4,
         scratch_shapes=[
-            vmem((tok, f), BF16), vmem((tok, d), BF16), vmem((4, sub, f), BF16), vmem((4, sub, f), BF16),
-            vmem((share, f), BF16), vmem((share, f), BF16), vmem((share, f), BF16), vmem((share, f), BF16),
-            dma((6,)), dma((4,)),
+            vmem((tok, f), BF16), vmem((tok, d), BF16), vmem((2, groups, half, ft), BF16), vmem((2, groups, half, ft), BF16),
+            vmem((2, half, f), BF16), vmem((2, half, f), BF16), vmem((2, half, f), BF16), vmem((2, half, f), BF16),
+            dma((2, 4)), dma((2,)), dma((6,)),
         ],
     )(placement[None, :], eo, tg, red, partner, weight[0], momentum[0])
     return eo, tg, nw[None], nm[None]

time: 149 us -> 150 us (level)
  no operation moved by 1% of the time
where the time goes in v1:
time: 150 us
  Pallas kernels  149 us (99%)
    pallas_call x1, Pallas kernels, shards(): pl.pallas_call(functools.partial(body, cfg), out_shape=results[:2] + (pie...  145 us
    pallas_call x1, Pallas kernels, shards(): pl.pallas_call(functools.partial(finish, n_dp), out_shape=results, in_spe...  3.76 us

profile of v1, /device:TPU:1, one launch (start us, length us, event | category | flops | bytes accessed | tf_op | source)
XLA Modules:
  0.0 150.0 jit_solution(9406622312786812177)
XLA Ops:
  0.6 145.4 %shard_map.102 = (bf16[128,1024]{1,0:T(8,128)(2,1)}, bf16[128,3584]{1,0:T(8,128)(2,1)}, bf16[2,4,112,256]{3,2,1,0:T(8,128)(2,1)}, bf16[2,4,112,256]{3,2,1,0:T(8,128)(2,1)}) custom-call(s32[1,128]{1,0:T(1,128)} %bitcast.10, f32[1,128]{1,0:T(1,128)} %bitcast.11, bf16[128,3584]{1,0:T(8,128)(2,1)} %tok_hbm.1, bf16[128,1024]{1,0:T(8,128)(2,1)} %cot_hbm.1, ...), custom_call_target="tpu_custom_call" | custom-call | tf_op jit(solution)/shard_map/pallas_call | solution.py:339
  146.1 3.8 %shard_map.103 = (bf16[128,1024]{1,0:T(8,128)(2,1)}, bf16[128,3584]{1,0:T(8,128)(2,1)}, bf16[224,1024]{1,0:T(8,128)(2,1)}, bf16[224,1024]{1,0:T(8,128)(2,1)}) custom-call(s32[1,48]{1,0:T(1,128)} %bitcast.12, bf16[128,1024]{1,0:T(8,128)(2,1)} %get-tuple-element.12.eo_in, bf16[128,3584]{1,0:T(8,128)(2,1)} %get-tuple-element.13.tg_in, ...), custom_call_target="tpu_custom_call" | custom-call | tf_op jit(solution)/shard_map/pallas_call | solution.py:364

commit v2 on v1

--- a/solution.py
+++ b/solution.py
@@ -55,10 +55,10 @@
 
 def body(
     cfg,
-    slot_hbm, rw_hbm, tok_hbm, cot_hbm, w_hbm,
+    slot_hbm, rw_hbm, place_hbm, tok_hbm, cot_hbm, w_hbm,
     eo_hbm, tg_hbm, red_hbm, pbuf,
-    slot_ref, rw_ref, tok_ref, cot_ref, eo_ref, tg_ref,
-    wv, stk, send, recv, bsend, brecv, xbuf, gbuf, gpbuf, actbuf, dw, pr, rbuf, red,
+    slot_ref, rw_ref, place_ref, tok_ref, cot_ref, eo_ref, tg_ref,
+    wv, stk, send, recv, bsend, brecv, xbuf, gbuf, gpbuf, actbuf, dw, pr, rbuf, red, redm,
     isem, wsem, osem, ssem, rsem, bssem, brsem, prs, prr, rss, rsr, ps, prv,
 ):
     plan = Plan(cfg["n_dp"], cfg["n_slots"])
@@ -87,13 +87,13 @@
     loads = [
         pltpu.make_async_copy(a, b, isem.at[i])
         for i, (a, b) in enumerate(
-            ((slot_hbm, slot_ref), (rw_hbm, rw_ref), (tok_hbm, tok_ref), (cot_hbm, cot_ref)))
+            ((slot_hbm, slot_ref), (rw_hbm, rw_ref), (place_hbm, place_ref), (tok_hbm, tok_ref), (cot_hbm, cot_ref)))
     ]
     for cp in loads:
         cp.start()
     w_copy = pltpu.make_async_copy(w_hbm, wv, wsem)
     w_copy.start()
-    for cp in loads[:2]:
+    for cp in loads[:3]:
         cp.wait()
 
     srow = slot_ref[...]
@@ -105,7 +105,7 @@
     upright = lambda row: jnp.sum(jnp.where(diag, row, 0.0), axis=1, keepdims=True)
     place_col = upright(place_row.astype(F32)).astype(jnp.int32)
     rw = upright(rw_ref[...])
-    for cp in loads[2:]:
+    for cp in loads[3:]:
         cp.wait()
     for q in range(QUARTERS):
         stk[q * tok:(q + 1) * tok, :dq] = tok_ref[:, q * dq:(q + 1) * dq]
@@ -198,6 +198,12 @@
     far = (plan.dp, (plan.me + n_slots // 2) % n_slots)
     pairs, hops, swaps, out_copies = {}, {}, [], []
 
+    labels = place_ref[...]
+    lane = iota(labels.shape, 1)
+    label = lambda s: jnp.sum(jnp.where(lane == s, labels, 0).astype(F32), axis=1, keepdims=True)
+    same = jnp.where(label(plan.me) == label(far[1]), 1.0, 0.0)
+    mask = jnp.broadcast_to(same, (half_rows, ft)) > 0.5
+
     def term(g):
         for q in range(QUARTERS):
             part = dot(xbuf[:, q * dq:(q + 1) * dq], gpbuf[:, g * ft:(g + 1) * ft], ((0,), (0,)))
@@ -226,10 +232,11 @@
                 hops[i, g, h] = cp
             else:
                 red[h, g] = val.astype(BF16)
+                redm[h, g] = jnp.where(mask, val, 0.0).astype(BF16)
                 out_copies.append(pltpu.make_async_copy(red.at[h, g], red_hbm.at[h, g], osem.at[2 + h * groups + g]))
                 out_copies[-1].start()
                 cp = pltpu.make_async_remote_copy(
-                    red.at[h, g], pbuf.at[h, g], ps.at[h, g], prv.at[h, g], device_id=far, device_id_type=MESH)
+                    redm.at[h, g], pbuf.at[h, g], ps.at[h, g], prv.at[h, g], device_id=far, device_id_type=MESH)
                 swaps.append(cp)
             cp.start()
 
@@ -271,12 +278,11 @@
 
 
 def finish(
-    n_dp,
-    place_ref, eo_in, tg_in, red_in, pbuf_in, w_hbm, mom_hbm,
+    eo_in, tg_in, red_in, pbuf_in, w_hbm, mom_hbm,
     eo_out, tg_out, nw_out, nm_out,
-    eov, tgv, redv, pbufv, wv, momv, nwv, nmv, isem, tsem, osem,
+    redv, pbufv, wv, momv, nwv, nmv, isem, osem,
 ):
-    dp, me, n_slots = lax.axis_index("dp"), lax.axis_index("expert"), place_ref.shape[1]
+    dp = lax.axis_index("dp")
     _, groups, half, ft = redv.shape
     row0 = dp * 2 * half
     ins = {}
@@ -286,36 +292,26 @@
             (red_in.at[h], redv.at[h]), (pbuf_in.at[h], pbufv.at[h]), (mom_hbm.at[pl.ds(h * half, half)], momv.at[h]), (old, wv.at[h]))):
             ins[h, j] = pltpu.make_async_copy(a, b, isem.at[h, j])
             ins[h, j].start()
-    whole = [pltpu.make_async_copy(a, b, tsem.at[i]) for i, (a, b) in enumerate(((tg_in, tgv), (eo_in, eov)))]
-    for cp in whole:
+    outs = [pltpu.make_async_copy(a, b, osem.at[i]) for i, (a, b) in enumerate(((tg_in, tg_out), (eo_in, eo_out)))]
+    for cp in outs:
         cp.start()
-    outs = [pltpu.make_async_copy(a, b, osem.at[i]) for i, (a, b) in enumerate(((tgv, tg_out), (eov, eo_out)))]
-    labels = place_ref[...]
-    lane = iota(labels.shape, 1)
-    label = lambda s: jnp.sum(jnp.where(lane == s, labels, 0).astype(F32), axis=1, keepdims=True)
-    same = jnp.where(label(me) == label((me + n_slots // 2) % n_slots), 1.0, 0.0)
-    mask = jnp.broadcast_to(same, (half, ft)) > 0.5
     for h in range(2):
         for j in range(4):
             ins[h, j].wait()
         for g in range(groups):
             cols = slice(g * ft, (g + 1) * ft)
-            total = redv[h, g].astype(F32) + jnp.where(mask, pbufv[h, g].astype(F32), 0.0)
+            total = redv[h, g].astype(F32) + pbufv[h, g].astype(F32)
             fresh = (DECAY_RATE * momv[h, :, cols].astype(F32) + total).astype(BF16)
             nmv[h, :, cols] = fresh
             nwv[h, :, cols] = (wv[h, :, cols].astype(F32) - LEARNING_RATE * fresh.astype(F32)).astype(BF16)
         for j, (a, b) in enumerate(((nmv, nm_out), (nwv, nw_out))):
             outs.append(pltpu.make_async_copy(a.at[h], b.at[pl.ds(h * half, half)], osem.at[2 + h * 2 + j]))
             outs[-1].start()
-        if h == 0:
-            for i in range(2):
-                whole[i].wait()
-                outs[i].start()
     for cp in outs:
         cp.wait()
 
 
-EARLY = True
+EARLY = False
 CHUNKS = ((0, 24), (24, 48))
 
 
@@ -331,7 +327,7 @@
     chunks = CHUNKS if n_slots == 48 else ((0, n_slots // 2), (n_slots // 2, n_slots))
     cfg = dict(n_dp=n_dp, n_slots=n_slots, chunks=chunks, ftile=ft)
     vmem, dma = pltpu.VMEM, pltpu.SemaphoreType.DMA
-    on_chip, anywhere = pl.BlockSpec(memory_space=pltpu.VMEM), pl.BlockSpec(memory_space=pl.ANY)
+    anywhere, in_hbm = pl.BlockSpec(memory_space=pl.ANY), pl.BlockSpec(memory_space=pltpu.HBM)
     slabs = (rows, QUARTERS, dq + fq)
     shape = jax.ShapeDtypeStruct
     pieces = shape((2, groups, half, ft), BF16)
@@ -339,10 +335,10 @@
     eo, tg, red, partner = pl.pallas_call(
         functools.partial(body, cfg),
         out_shape=results[:2] + (pieces, pieces),
-        in_specs=[anywhere] * 5,
+        in_specs=[in_hbm] * 6,
         out_specs=(anywhere,) * 4,
         scratch_shapes=[
-            vmem((1, tok), jnp.int32), vmem((1, tok), F32),
+            vmem((1, tok), jnp.int32), vmem((1, tok), F32), vmem((1, n_slots), jnp.int32),
             vmem((tok, d), BF16), vmem((tok, f), BF16), vmem((tok, f), BF16), vmem((tok, d), BF16),
             vmem((d, f), BF16),
             vmem((QUARTERS * max(rows, tok), dq + fq), BF16),
@@ -352,26 +348,27 @@
             vmem((groups, n_dp * 2, half, ft), BF16),
             vmem((groups, ny, 2, half, ft), BF16),
             vmem((groups, ny - 1, 2, half, ft), BF16),
-            vmem((2, groups, half, ft), BF16),
-            dma((4,)), dma, dma((2 + 2 * groups,)), dma, dma((len(chunks),)), dma, dma,
+            vmem((2, groups, half, ft), BF16), vmem((2, groups, half, ft), BF16),
+            dma((5,)), dma, dma((2 + 2 * groups,)), dma, dma((len(chunks),)), dma, dma,
             dma((groups, ny, 2)), dma((groups, ny, 2)),
             dma((groups, ny - 1, 2)), dma((groups, ny - 1, 2)),
             dma((2, groups)), dma((2, groups)),
         ],
         compiler_params=pltpu.CompilerParams(
-            collective_id=0, has_side_effects=True, vmem_limit_bytes=60 * 1024 * 1024),
-    )(slot_ids[None, :], route_weight[None, :], tokens, cotangent, weight[0])
+            collective_id=0, has_side_effects=True, vmem_limit_bytes=48 * 1024 * 1024),
+    )(slot_ids[None, :], route_weight[None, :], placement[None, :], tokens, cotangent, weight[0])
     eo, tg, nw, nm = pl.pallas_call(
-        functools.partial(finish, n_dp),
+        finish,
         out_shape=results,
-        in_specs=[on_chip] + [anywhere] * 6,
-        out_specs=(anywhere,) * 4,
+        in_specs=[anywhere] * 4 + [in_hbm, anywhere],
+        out_specs=(in_hbm,) * 4,
         scratch_shapes=[
-            vmem((tok, f), BF16), vmem((tok, d), BF16), vmem((2, groups, half, ft), BF16), vmem((2, groups, half, ft), BF16),
+            vmem((2, groups, half, ft), BF16), vmem((2, groups, half, ft), BF16),
             vmem((2, half, f), BF16), vmem((2, half, f), BF16), vmem((2, half, f), BF16), vmem((2, half, f), BF16),
-            dma((2, 4)), dma((2,)), dma((6,)),
+            dma((2, 4)), dma((6,)),
         ],
-    )(placement[None, :], eo, tg, red, partner, weight[0], momentum[0])
+        compiler_params=pltpu.CompilerParams(vmem_limit_bytes=12 * 1024 * 1024),
+    )(eo, tg, red, partner, weight[0], momentum[0])
     return eo, tg, nw[None], nm[None]
 
 

time: 150 us -> 154 us (1.027)
  local copies, waits for them, and re-layouts: 0 us -> 4.47 us
    unnamed x0 -> x14, local copies, waits for them, and re-layouts: none -> 4.47 us
where the time goes in v2:
time: 154 us
  Pallas kernels  148 us (96%)
  local copies, waits for them, and re-layouts  4.47 us (3%)
    pallas_call x1, Pallas kernels, shards(): pl.pallas_call(functools.partial(body, cfg), out_shape=results[:2] + (pie...  145 us
    unnamed x14, local copies, waits for them, and re-layouts  4.47 us
    pallas_call x1, Pallas kernels, shards(): pl.pallas_call(finish, out_shape=results, in_specs=[anywhere] * 4 + [in_h...  3.8 us

profile of v2, /device:TPU:1, one launch (start us, length us, event | category | flops | bytes accessed | tf_op | source)
XLA Modules:
  0.0 153.7 jit_solution(8277994797764035286)
XLA Ops:
  0.6 0.0 copy-start
  0.6 0.0 copy-start.1
  0.7 1.3 copy-done.1
  2.0 0.0 copy-start.3
  2.0 1.2 copy-done.3
  3.1 0.0 copy-start.4
  3.1 0.7 copy-done.4
  3.8 0.0 copy-start.5
  3.8 0.7 copy-done.5
  4.5 0.0 copy-start.6
  4.5 0.7 copy-done.6
  5.1 0.0 copy-start.2
  5.1 144.6 %shard_map.102 = (bf16[128,1024]{1,0:T(8,128)(2,1)S(1)}, bf16[128,3584]{1,0:T(8,128)(2,1)S(1)}, bf16[2,4,112,256]{3,2,1,0:T(8,128)(2,1)S(1)}, bf16[2,4,112,256]{3,2,1,0:T(8,128)(2,1)S(1)}) custom-call(s32[1,128]{1,0:T(1,128)S(1)} %bitcast.10, f32[1,128]{1,0:T(1,128)S(1)} %bitcast.11, s32[1,48]{1,0:T(1,128)S(1)} %bitcast.12, bf16[128,3584]{1,0:T(8,128)(2,1)S(1)} %copy-done.1, ...), custom_call_target="tpu_custom_call" | custom-call | tf_op jit(solution)/shard_map/pallas_call | solution.py:335
  149.7 0.0 copy-done
  149.7 0.0 copy-done.2
  149.7 3.8 %shard_map.103 = (bf16[128,1024]{1,0:T(8,128)(2,1)}, bf16[128,3584]{1,0:T(8,128)(2,1)}, bf16[224,1024]{1,0:T(8,128)(2,1)}, bf16[224,1024]{1,0:T(8,128)(2,1)}) custom-call(bf16[128,1024]{1,0:T(8,128)(2,1)S(1)} %get-tuple-element.12.eo_in, bf16[128,3584]{1,0:T(8,128)(2,1)S(1)} %get-tuple-element.13.tg_in, ...), custom_call_target="tpu_custom_call" | custom-call | tf_op jit(solution)/shard_map/pallas_call | solution.py:360
Async XLA Ops:
  0.6 149.1 %copy-start = (bf16[1,3584,1024]{2,1,0:T(8,128)(2,1)S(1)}, bf16[1,3584,1024]{2,1,0:T(8,128)(2,1)}, u32[]{:S(2)}) copy-start(bf16[1,3584,1024]{2,1,0:T(8,128)(2,1)} %param.12) | copy-start | bytes 22020100
  0.6 1.3 copy-start.1
  2.0 1.2 copy-start.3
  3.1 0.7 copy-start.4
  3.8 0.7 copy-start.5
  4.5 0.7 copy-start.6
  5.1 144.6 %copy-start.2 = (bf16[1,224,1024]{2,1,0:T(8,128)(2,1)S(1)}, bf16[1,224,1024]{2,1,0:T(8,128)(2,1)}, u32[]{:S(2)}) copy-start(bf16[1,224,1024]{2,1,0:T(8,128)(2,1)} %param.13) | copy-start | bytes 1376260

commit v3 on v2

--- a/solution.py
+++ b/solution.py
@@ -280,7 +280,7 @@
 def finish(
     eo_in, tg_in, red_in, pbuf_in, w_hbm, mom_hbm,
     eo_out, tg_out, nw_out, nm_out,
-    redv, pbufv, wv, momv, nwv, nmv, isem, osem,
+    eov, tgv, redv, pbufv, wv, momv, nwv, nmv, isem, tsem, osem,
 ):
     dp = lax.axis_index("dp")
     _, groups, half, ft = redv.shape
@@ -292,9 +292,10 @@
             (red_in.at[h], redv.at[h]), (pbuf_in.at[h], pbufv.at[h]), (mom_hbm.at[pl.ds(h * half, half)], momv.at[h]), (old, wv.at[h]))):
             ins[h, j] = pltpu.make_async_copy(a, b, isem.at[h, j])
             ins[h, j].start()
-    outs = [pltpu.make_async_copy(a, b, osem.at[i]) for i, (a, b) in enumerate(((tg_in, tg_out), (eo_in, eo_out)))]
-    for cp in outs:
+    whole = [pltpu.make_async_copy(a, b, tsem.at[i]) for i, (a, b) in enumerate(((tg_in, tgv), (eo_in, eov)))]
+    for cp in whole:
         cp.start()
+    outs = [pltpu.make_async_copy(a, b, osem.at[i]) for i, (a, b) in enumerate(((tgv, tg_out), (eov, eo_out)))]
     for h in range(2):
         for j in range(4):
             ins[h, j].wait()
@@ -307,6 +308,10 @@
         for j, (a, b) in enumerate(((nmv, nm_out), (nwv, nw_out))):
             outs.append(pltpu.make_async_copy(a.at[h], b.at[pl.ds(h * half, half)], osem.at[2 + h * 2 + j]))
             outs[-1].start()
+        if h == 0:
+            for i in range(2):
+                whole[i].wait()
+                outs[i].start()
     for cp in outs:
         cp.wait()
 
@@ -327,7 +332,7 @@
     chunks = CHUNKS if n_slots == 48 else ((0, n_slots // 2), (n_slots // 2, n_slots))
     cfg = dict(n_dp=n_dp, n_slots=n_slots, chunks=chunks, ftile=ft)
     vmem, dma = pltpu.VMEM, pltpu.SemaphoreType.DMA
-    anywhere, in_hbm = pl.BlockSpec(memory_space=pl.ANY), pl.BlockSpec(memory_space=pltpu.HBM)
+    anywhere = pl.BlockSpec(memory_space=pl.ANY)
     slabs = (rows, QUARTERS, dq + fq)
     shape = jax.ShapeDtypeStruct
     pieces = shape((2, groups, half, ft), BF16)
@@ -335,7 +340,7 @@
     eo, tg, red, partner = pl.pallas_call(
         functools.partial(body, cfg),
         out_shape=results[:2] + (pieces, pieces),
-        in_specs=[in_hbm] * 6,
+        in_specs=[anywhere] * 6,
         out_specs=(anywhere,) * 4,
         scratch_shapes=[
             vmem((1, tok), jnp.int32), vmem((1, tok), F32), vmem((1, n_slots), jnp.int32),
@@ -355,19 +360,18 @@
             dma((2, groups)), dma((2, groups)),
         ],
         compiler_params=pltpu.CompilerParams(
-            collective_id=0, has_side_effects=True, vmem_limit_bytes=48 * 1024 * 1024),
+            collective_id=0, has_side_effects=True, vmem_limit_bytes=60 * 1024 * 1024),
     )(slot_ids[None, :], route_weight[None, :], placement[None, :], tokens, cotangent, weight[0])
     eo, tg, nw, nm = pl.pallas_call(
         finish,
         out_shape=results,
-        in_specs=[anywhere] * 4 + [in_hbm, anywhere],
-        out_specs=(in_hbm,) * 4,
+        in_specs=[anywhere] * 6,
+        out_specs=(anywhere,) * 4,
         scratch_shapes=[
-            vmem((2, groups, half, ft), BF16), vmem((2, groups, half, ft), BF16),
+            vmem((tok, f), BF16), vmem((tok, d), BF16), vmem((2, groups, half, ft), BF16), vmem((2, groups, half, ft), BF16),
             vmem((2, half, f), BF16), vmem((2, half, f), BF16), vmem((2, half, f), BF16), vmem((2, half, f), BF16),
-            dma((2, 4)), dma((6,)),
+            dma((2, 4)), dma((2,)), dma((6,)),
         ],
-        compiler_params=pltpu.CompilerParams(vmem_limit_bytes=12 * 1024 * 1024),
     )(eo, tg, red, partner, weight[0], momentum[0])
     return eo, tg, nw[None], nm[None]
 

time: 154 us -> 149 us (0.968)
  local copies, waits for them, and re-layouts: 4.47 us -> 0 us
    unnamed x14 -> x0, local copies, waits for them, and re-layouts: 4.47 us -> none
where the time goes in v3:
time: 149 us; the launch traced here: 148 us
  Pallas kernels  148 us (99%)
    pallas_call x1, Pallas kernels, shards(): pl.pallas_call(functools.partial(body, cfg), out_shape=results[:2] + (pie...  144 us
    pallas_call x1, Pallas kernels, shards(): pl.pallas_call(finish, out_shape=results, in_specs=[anywhere] * 6, out_sp...  3.19 us

profile of v3, /device:TPU:1, one launch (start us, length us, event | category | flops | bytes accessed | tf_op | source)
XLA Modules:
  0.0 148.4 jit_solution(15086233564491603030)
XLA Ops:
  0.6 144.4 %shard_map.102 = (bf16[128,1024]{1,0:T(8,128)(2,1)}, bf16[128,3584]{1,0:T(8,128)(2,1)}, bf16[2,4,112,256]{3,2,1,0:T(8,128)(2,1)}, bf16[2,4,112,256]{3,2,1,0:T(8,128)(2,1)}) custom-call(s32[1,128]{1,0:T(1,128)} %bitcast.10, f32[1,128]{1,0:T(1,128)} %bitcast.11, s32[1,48]{1,0:T(1,128)} %bitcast.12, bf16[128,3584]{1,0:T(8,128)(2,1)} %tok_hbm.1, ...), custom_call_target="tpu_custom_call" | custom-call | tf_op jit(solution)/shard_map/pallas_call | solution.py:340
  145.1 3.2 %shard_map.103 = (bf16[128,1024]{1,0:T(8,128)(2,1)}, bf16[128,3584]{1,0:T(8,128)(2,1)}, bf16[224,1024]{1,0:T(8,128)(2,1)}, bf16[224,1024]{1,0:T(8,128)(2,1)}) custom-call(bf16[128,1024]{1,0:T(8,128)(2,1)} %get-tuple-element.12.eo_in, bf16[128,3584]{1,0:T(8,128)(2,1)} %get-tuple-element.13.tg_in, bf16[2,4,112,256]{3,2,1,0:T(8,128)(2,1)} %get-tuple-element.14.red_in, ...), custom_call_target="tpu_custom_call" | custom-call | tf_op jit(solution)/shard_map/pallas_call | solution.py:365
